TPU v7x, 256 devices: a whole 4x4x8 slice. The times are simulated.
256 devices in a mesh: seq: 16 (over z, x_lo), head: 4 (over x_hi, core), req: 4 (over y).
Axes of the slice: x: 4 (x_hi: 2, x_lo: 2; x = x_hi * 2 + x_lo), y: 4, z: 8, core: 2. Of those that a mesh axis runs over, the one named last changes fastest.
Arguments:
- queries: bfloat16 [32768, 2560], P(('req', 'seq'), 'head'), parts along dimension 0, may hold values from -8 to 8
- keys: bfloat16 [32768, 2560], P(('req', 'seq'), 'head'), parts along dimension 0, may hold values from -8 to 8
- values: bfloat16 [32768, 2560], P(('req', 'seq'), 'head'), parts along dimension 0, may hold values from -8 to 8
- clip_ids: int32 [32768], P('req'), parts along dimension 0, may hold values from 0 to 3, never falling along the last dimension, each value on 1 to 3072 neighbouring positions
- plan: int32 [256], P('req'), parts along dimension 0, may hold values from 0 to 15, as said below
Outputs:
- attended: bfloat16 [32768, 2560], P(('req', 'seq'), 'head'), parts along dimension 0
- log_normalizer: float32 [20, 32768], P('head', ('req', 'seq')), parts along dimension 1
There are 4 independent parts, one for each index of `req`. A program takes and returns all parts, laid end to end along the dimension named above; each array names one. Nothing has to cross between parts.
Inputs may be any that keep to these rules, and one draw needn't show every extreme that they name: `plan`: every index along seq computes exactly 4 blocks, and of the 4 blocks held by one index of seq (blocks k * 4 to k * 4 + 3 on index k) at most 1 go to the same index; some pair of indices reaches 1. `clip_ids`: clip ids never fall along the tokens; each clip holds 1 to 3072 tokens and one holds exactly 3072.
All inputs are finite; a program needn't handle non-finite values.
Results may differ from a plain program's by a relative error of at most 0.007.
Values may be sent and summed in bfloat16 or wider, within the bound.
A program may use at most 128 MiB of HBM per device.

v0:
```python
import jax
import jax.numpy as jnp
from jax import lax
from jax.sharding import PartitionSpec as P

HD = 128
BLOCK = 128


def shards(queries, keys, values, clip_ids, plan):
    group_size = lax.axis_size("seq")
    rank_here = lax.axis_index("seq")
    tok_dev, width_dev = queries.shape
    blocks_dev = tok_dev // BLOCK
    blocks_all = plan.shape[0]
    capacity = (blocks_dev + group_size - 1) // group_size
    slot_count = group_size * capacity
    heads_dev = width_dev // HD
    score_scale = 1.0 / HD**0.5
    block_index = jnp.arange(blocks_all, dtype=jnp.int32)
    source = block_index // blocks_dev
    earlier = (
        (plan[None, :] == plan[:, None])
        & (source[None, :] == source[:, None])
        & (block_index[None, :] < block_index[:, None])
    )
    pair_rank = jnp.sum(earlier, axis=1)
    send_slot = plan * capacity + pair_rank
    recv_slot_all = source * capacity + pair_rank
    local_send = lax.dynamic_slice_in_dim(send_slot, rank_here * blocks_dev, blocks_dev)
    slot_range = jnp.arange(slot_count, dtype=jnp.int32)
    local_range = jnp.arange(blocks_dev, dtype=jnp.int32)
    send_match = slot_range[:, None] == local_send[None, :]
    send_pick = jnp.sum(send_match * local_range[None, :], axis=1)
    send_filled = jnp.any(send_match, axis=1)
    owned_here = plan == rank_here
    position = jnp.cumsum(owned_here.astype(jnp.int32)) - 1
    choose = (local_range[:, None] == position[None, :]) & owned_here[None, :]
    recv_pick = jnp.sum(choose * recv_slot_all[None, :], axis=1)
    back_match = slot_range[:, None] == recv_pick[None, :]
    back_pick = jnp.sum(back_match * local_range[None, :], axis=1)
    back_filled = jnp.any(back_match, axis=1)
    sort_key = plan * blocks_all + block_index
    packed_place = jnp.sum(sort_key[None, :] < sort_key[:, None], axis=1)
    packed_block = jnp.sum(
        (packed_place[None, :] == block_index[:, None]) * block_index[None, :], axis=1
    )
    packed_ids = jnp.take(clip_ids.reshape(blocks_all, BLOCK), packed_block, axis=0).reshape(-1)

    def pack_slots(tokens_dev, picked, filled):
        columns = tokens_dev.shape[1]
        blocked = jnp.take(tokens_dev.reshape(blocks_dev, BLOCK, columns), picked, axis=0)
        blocked = jnp.where(filled[:, None, None], blocked, jnp.zeros_like(blocked))
        return blocked.reshape(group_size, capacity, BLOCK, columns)

    def read_slots(arrived, picked):
        columns = arrived.shape[-1]
        blocked = jnp.take(arrived.reshape(slot_count, BLOCK, columns), picked, axis=0)
        return blocked.reshape(blocks_dev * BLOCK, columns)

    arrived = (
        lax.all_to_all(
            pack_slots(queries, send_pick, send_filled),
            "seq",
            split_axis=0,
            concat_axis=0,
            tiled=True,
        ),
        lax.all_to_all(
            pack_slots(keys, send_pick, send_filled), "seq", split_axis=0, concat_axis=0, tiled=True
        ),
        lax.all_to_all(
            pack_slots(values, send_pick, send_filled),
            "seq",
            split_axis=0,
            concat_axis=0,
            tiled=True,
        ),
    )
    query_rows = read_slots(arrived[0], recv_pick)
    loop_source = (read_slots(arrived[1], recv_pick), read_slots(arrived[2], recv_pick))
    query_ids = lax.dynamic_slice_in_dim(packed_ids, rank_here * tok_dev, tok_dev)
    query_heads = query_rows.reshape(tok_dev, heads_dev, HD)

    def attend_block(state, key_part, value_part, part_ids):
        running_max, running_sum, accumulated = state
        rows = key_part.shape[0]
        scores = (
            jnp.einsum(
                "qhd,khd->hqk",
                query_heads,
                key_part.reshape(rows, heads_dev, HD),
                preferred_element_type=jnp.float32,
            )
            * score_scale
        )
        same_clip = (query_ids[:, None] == part_ids[None, :])[None, :, :]
        masked = jnp.where(same_clip, scores, jnp.float32(-1e30))
        new_max = jnp.maximum(running_max, jnp.max(masked, axis=2))
        weights = jnp.where(same_clip, jnp.exp(masked - new_max[:, :, None]), jnp.float32(0.0))
        rescale = jnp.exp(running_max - new_max)
        running_sum = running_sum * rescale + jnp.sum(weights, axis=2)
        product = jnp.einsum(
            "hqk,khd->qhd",
            weights.astype(jnp.bfloat16),
            value_part.reshape(rows, heads_dev, HD),
            preferred_element_type=jnp.float32,
        )
        accumulated = accumulated * jnp.transpose(rescale)[:, :, None] + product
        return (new_max, running_sum, accumulated)

    start_state = (
        jnp.full((heads_dev, tok_dev), -1e30, jnp.float32),
        jnp.zeros((heads_dev, tok_dev), jnp.float32),
        jnp.zeros((tok_dev, heads_dev, HD), jnp.float32),
    )
    key_part = lax.all_gather(loop_source[0], "seq", axis=0, tiled=True)
    value_part = lax.all_gather(loop_source[1], "seq", axis=0, tiled=True)
    part_ids = packed_ids
    rows = key_part.shape[0]
    sub_count = rows // 512

    def scan_step(inner_state, inputs):
        return (attend_block(inner_state, inputs[0], inputs[1], inputs[2]), None)

    inputs = (
        key_part.reshape(sub_count, 512, width_dev),
        value_part.reshape(sub_count, 512, width_dev),
        part_ids.reshape(sub_count, 512),
    )
    final_state, unused = lax.scan(scan_step, start_state, inputs)
    running_max, running_sum, accumulated = final_state
    finished = (
        (accumulated / jnp.transpose(running_sum)[:, :, None])
        .astype(jnp.bfloat16)
        .reshape(tok_dev, width_dev)
    )
    log_totals = running_max + jnp.log(running_sum)
    returned = lax.all_to_all(
        pack_slots(finished, back_pick, back_filled), "seq", split_axis=0, concat_axis=0, tiled=True
    )
    attended = read_slots(returned, local_send)
    return (attended, log_totals)


def solution(mesh):
    return jax.shard_map(
        shards,
        mesh=mesh,
        in_specs=(
            P(("req", "seq"), "head"),
            P(("req", "seq"), "head"),
            P(("req", "seq"), "head"),
            P("req"),
            P("req"),
        ),
        out_specs=(P(("req", "seq"), "head"), P("head", ("req", "seq"))),
        check_vma=False,
    )
```

profile of v0, /device:TPU:4, one launch (start us, length us, event | category | flops | bytes accessed | tf_op | source)
XLA Modules:
  0.0 998.7 jit_solution(18444506933324885968)
XLA Ops:
  21.4 71.3 %all_to_all.20 = bf16[16,1,128,640]{3,2,1,0:T(8,128)(2,1)} all-to-all(bf16[16,1,128,640]{3,2,1,0:T(8,128)(2,1)S(1)} %get-tuple-element.152), channel_id=1, replica_groups=mesh['seq'=16,'head'=4,'req'=4] {'seq'}, dimensions={0} | all-to-all | bytes 5242880 | tf_op jit(solution)/shard_map/all_to_all | solution.py:69
  92.7 65.1 %all_to_all.21 = bf16[16,1,128,640]{3,2,1,0:T(8,128)(2,1)} all-to-all(bf16[16,1,128,640]{3,2,1,0:T(8,128)(2,1)S(1)} %get-tuple-element.151), channel_id=1, replica_groups=mesh['seq'=16,'head'=4,'req'=4] {'seq'}, dimensions={0} | all-to-all | bytes 5242880 | tf_op jit(solution)/shard_map/all_to_all | solution.py:62
  168.7 53.8 %all-to-all-done.2 = bf16[16,1,128,640]{3,2,1,0:T(8,128)(2,1)S(1)} async-done(((bf16[16,1,128,640]{3,2,1,0:T(8,128)(2,1)}), bf16[16,1,128,640]{3,2,1,0:T(8,128)(2,1)S(1)}, u32[]{:S(2)}, u32[]{:S(2)}) %all-to-all-start.2) | async-done | bytes 2621472 | tf_op jit(solution)/shard_map/all_to_all | solution.py:72
  232.9 216.5 %all-gather.3.cloned.1.call-done = bf16[8192,640]{1,0:T(8,128)(2,1)} async-done(((bf16[512,640]{1,0:T(8,128)(2,1)}), bf16[8192,640]{1,0:T(8,128)(2,1)}) %all-gather.3.cloned.1.call-update) | async-done | bytes 10485776 | tf_op jit(solution)/shard_map/all_gather | solution.py:117
  449.4 227.8 %all-gather.5.cloned.1.call-done = bf16[8192,640]{1,0:T(8,128)(2,1)} async-done(((bf16[512,640]{1,0:T(8,128)(2,1)}), bf16[8192,640]{1,0:T(8,128)(2,1)}) %all-gather.5.cloned.1.call-update) | async-done | bytes 10485776 | tf_op jit(solution)/shard_map/all_gather | solution.py:118
  677.2 236.1 %while.15 = (s32[]{:T(128)}, f32[5,512]{1,0:T(8,128)S(1)}, f32[5,512]{1,0:T(8,128)}, f32[512,5,128]{0,2,1:T(8,128)}, s32[512]{0:T(512)}, /*index=5*/s32[16,512]{...) while((s32[]{:T(128)}, f32[5,512]{1,0:T(8,128)S(1)}, ...), condition=%wide.region_11.14_spmd.clone, body=%wide.region_8.0_spmd.clone.sunk | while | flops 689388544 | bytes 42590440 | solution.py:131
  684.3 5.4 fusion.47
  698.7 5.8 fusion.47
  713.5 5.8 fusion.47
  728.3 5.8 fusion.47
  743.0 5.8 fusion.47
  757.8 5.8 fusion.47
  772.6 5.8 fusion.47
  787.4 5.8 fusion.47
  802.1 5.8 fusion.47
  816.9 5.8 fusion.47
  831.7 5.8 fusion.47
  846.5 5.8 fusion.47
  861.3 5.8 fusion.47
  876.0 5.8 fusion.47
  890.8 5.8 fusion.47
  905.6 5.8 fusion.47
  919.0 7.6 all-to-all-start.3
  927.2 61.1 %all-to-all-done.3 = bf16[16,1,128,640]{3,2,1,0:T(8,128)(2,1)S(1)} async-done(((bf16[16,1,128,640]{3,2,1,0:T(8,128)(2,1)}), bf16[16,1,128,640]{3,2,1,0:T(8,128)(2,1)S(1)}, u32[]{:S(2)}, u32[]{:S(2)}) %all-to-all-start.3) | async-done | bytes 2621472 | tf_op jit(solution)/shard_map/all_to_all | solution.py:139
  (393 shorter events, 187.5 us)
Async XLA Ops:
  157.8 64.7 %all-to-all-start.2 = ((bf16[16,1,128,640]{3,2,1,0:T(8,128)(2,1)}), bf16[16,1,128,640]{3,2,1,0:T(8,128)(2,1)S(1)}, u32[]{:S(2)}, u32[]{:S(2)}) async-start(bf16[16,1,128,640]{3,2,1,0:T(8,128)(2,1)} %get-tuple-element.150), calls=%async_computation.2 | async-start | bytes 5242880 | tf_op jit(solution)/shard_map/all_to_all | solution.py:72
  161.7 287.7 %all-gather.3.cloned.1.call-start = ((), (), s32[]{:S(2)}) async-start(), calls=%async_computation.4 | async-start | bytes 11141120 | tf_op jit(solution)/shard_map/all_gather | solution.py:117
  226.8 450.4 %all-gather.5.cloned.1.call-start = ((), (), s32[]{:S(2)}) async-start(), calls=%async_computation.5 | async-start | bytes 11141120 | tf_op jit(solution)/shard_map/all_gather | solution.py:118
  698.4 6.1 slice-start
  698.7 5.8 slice-start.1
  713.2 6.1 slice-start
  728.0 6.1 slice-start
  742.7 6.1 slice-start
  757.5 6.1 slice-start
  772.3 6.1 slice-start
  787.1 6.1 slice-start
  801.9 6.1 slice-start
  816.6 6.1 slice-start
  831.4 6.1 slice-start
  846.2 6.1 slice-start
  861.0 6.1 slice-start
  875.8 6.1 slice-start
  890.5 6.1 slice-start
  905.3 6.1 slice-start
  919.0 7.6 copy-start.14
  919.0 7.6 copy-start.8
  919.0 70.8 %copy-start.10 = (pred[4]{0:T(512)(128)(4,1)S(1)}, pred[4]{0:T(512)(128)(4,1)}, u32[]{:S(2)}) copy-start(pred[4]{0:T(512)(128)(4,1)} %get-tuple-element.142) | copy-start | bytes 16
  919.0 69.4 %all-to-all-start.3 = ((bf16[16,1,128,640]{3,2,1,0:T(8,128)(2,1)}), bf16[16,1,128,640]{3,2,1,0:T(8,128)(2,1)S(1)}, u32[]{:S(2)}, u32[]{:S(2)}) async-start(bf16[16,1,128,640]{3,2,1,0:T(8,128)(2,1)} %fusion.17), calls=%async_computation.3 | async-start | bytes 5242880 | tf_op jit(solution)/shard_map/all_to_all | solution.py:139
  926.6 65.3 %copy-start.1 = (bf16[512,640]{1,0:T(8,128)(2,1)S(1)}, bf16[512,640]{1,0:T(8,128)(2,1)}, u32[]{:S(2)}) copy-start(bf16[512,640]{1,0:T(8,128)(2,1)} %param.11) | copy-start | bytes 1966084
  (57 other events, 143.3 us)
Sparse Core Ops, SparseCore 0:
  227.0 222.3 all-gather.2
  451.8 225.4 all-gather.4
where the time goes:
time: 1000 us; the launch traced here: 999 us
  waiting for transfers between devices  560 us (56%)
  matrix products  148 us (15%)
  blocking collectives  136 us (14%)
  local copies, waits for them, and re-layouts  73.1 us (7%)
  other arithmetic  54 us (5%)
  between operations  14.3 us (1%)
  starting transfers between devices  11.5 us (1%)
    all_gather x1, waiting for transfers between devices, shards(): value_part = lax.all_gather(loop_source[1], 'seq', axis=0, tiled=True)  228 us
    all_gather x1, waiting for transfers between devices, shards(): key_part = lax.all_gather(loop_source[0], 'seq', axis=0, tiled=True)  217 us
    dot_general x16, matrix products, attend_block(): jnp.einsum('hqk,khd->qhd', weights.astype(jnp.bfloat16), value_part.resha...  92 us
    all_to_all x1, blocking collectives, shards(): lax.all_to_all(pack_slots(keys, send_pick, send_filled), 'seq', split_axi...  71.3 us
    all_to_all x1, blocking collectives, shards(): lax.all_to_all(pack_slots(queries, send_pick, send_filled), 'seq', split_...  65.1 us
    all_to_all x1, waiting for transfers between devices, shards(): lax.all_to_all(pack_slots(finished, back_pick, back_filled), 'seq', split...  61.1 us
    dot_general x16, matrix products, attend_block(): jnp.einsum('qhd,khd->hqk', query_heads, key_part.reshape(rows, heads_dev,...  55.7 us
    all_to_all x1, waiting for transfers between devices, shards(): lax.all_to_all(pack_slots(values, send_pick, send_filled), 'seq', split_a...  53.8 us
  transfers between devices with their start and end apart: 4, of which 4 were waited for; matrix products, arithmetic and copies ran while one was open for 1% of the time, Pallas kernels for 0%

commit v1 on v0

--- a/solution.py
+++ b/solution.py
@@ -115,7 +115,11 @@
         jnp.zeros((tok_dev, heads_dev, HD), jnp.float32),
     )
     key_part = lax.all_gather(loop_source[0], "seq", axis=0, tiled=True)
-    value_part = lax.all_gather(loop_source[1], "seq", axis=0, tiled=True)
+    block = loop_source[1]
+    peers = lax.axis_size("seq")
+    pieces = jnp.stack([block for _ in range(peers)])
+    pieces = lax.all_to_all(pieces, "seq", split_axis=0, concat_axis=0)
+    value_part = jnp.concatenate(pieces, axis=0)
     part_ids = packed_ids
     rows = key_part.shape[0]
     sub_count = rows // 512

time: 1000 us -> 917 us (0.917)
  waiting for transfers between devices: 560 us -> 499 us
  matrix products: 148 us -> 128 us
  other arithmetic: 54 us -> 40 us
    all_to_all x0 -> x1, waiting for transfers between devices: none -> 284 us  [shards(): pieces = lax.all_to_all(pieces, 'seq', split_axis=0, concat_axis=0)]
    all_gather x1 -> x0, waiting for transfers between devices: 228 us -> none  [shards(): value_part = lax.all_gather(loop_source[1], 'seq', axis=0, tiled=True)]
    all_gather x1, waiting for transfers between devices: 217 us -> 101 us  [shards(): key_part = lax.all_gather(loop_source[0], 'seq', axis=0, tiled=True)]
    dot_general x16, matrix products: 92 us -> 72.3 us  [attend_block(): jnp.einsum('hqk,khd->qhd', weights.astype(jnp.bfloat16), value_part.resha...]
    eq x16, other arithmetic: 14.3 us -> 3.42 us  [attend_block(): same_clip = (query_ids[:, None] == part_ids[None, :])[None, :, :]]
where the time goes in v1:
time: 917 us; the launch traced here: 908 us
  waiting for transfers between devices  499 us (54%)
  blocking collectives  136 us (15%)
  matrix products  128 us (14%)
  local copies, waits for them, and re-layouts  69.1 us (8%)
  other arithmetic  40 us (4%)
  starting transfers between devices  18.2 us (2%)
  between operations  14.3 us (2%)
    all_to_all x1, waiting for transfers between devices, shards(): pieces = lax.all_to_all(pieces, 'seq', split_axis=0, concat_axis=0)  284 us
    all_gather x1, waiting for transfers between devices, shards(): key_part = lax.all_gather(loop_source[0], 'seq', axis=0, tiled=True)  101 us
    dot_general x16, matrix products, attend_block(): jnp.einsum('hqk,khd->qhd', weights.astype(jnp.bfloat16), value_part.resha...  72.3 us
    all_to_all x1, blocking collectives, shards(): lax.all_to_all(pack_slots(keys, send_pick, send_filled), 'seq', split_axi...  71.3 us
    all_to_all x1, blocking collectives, shards(): lax.all_to_all(pack_slots(queries, send_pick, send_filled), 'seq', split_...  65.1 us
    all_to_all x1, waiting for transfers between devices, shards(): lax.all_to_all(pack_slots(finished, back_pick, back_filled), 'seq', split...  60 us
    dot_general x16, matrix products, attend_block(): jnp.einsum('qhd,khd->hqk', query_heads, key_part.reshape(rows, heads_dev,...  55.7 us
    all_to_all x1, waiting for transfers between devices, shards(): lax.all_to_all(pack_slots(values, send_pick, send_filled), 'seq', split_a...  53.9 us
  transfers between devices with their start and end apart: 4, of which 4 were waited for; matrix products, arithmetic and copies ran while one was open for 1% of the time, Pallas kernels for 0%

profile of v1, /device:TPU:4, one launch (start us, length us, event | category | flops | bytes accessed | tf_op | source)
XLA Modules:
  0.0 907.9 jit_solution(11370876937812873643)
XLA Ops:
  20.5 71.3 %all_to_all.25 = bf16[16,1,128,640]{3,2,1,0:T(8,128)(2,1)} all-to-all(bf16[16,1,128,640]{3,2,1,0:T(8,128)(2,1)S(1)} %get-tuple-element.150), channel_id=1, replica_groups=mesh['seq'=16,'head'=4,'req'=4] {'seq'}, dimensions={0} | all-to-all | bytes 5242880 | tf_op jit(solution)/shard_map/all_to_all | solution.py:69
  91.9 65.1 %all_to_all.26 = bf16[16,1,128,640]{3,2,1,0:T(8,128)(2,1)} all-to-all(bf16[16,1,128,640]{3,2,1,0:T(8,128)(2,1)S(1)} %get-tuple-element.149), channel_id=1, replica_groups=mesh['seq'=16,'head'=4,'req'=4] {'seq'}, dimensions={0} | all-to-all | bytes 5242880 | tf_op jit(solution)/shard_map/all_to_all | solution.py:62
  167.8 53.9 %all-to-all-done.2 = bf16[16,1,128,640]{3,2,1,0:T(8,128)(2,1)S(1)} async-done(((bf16[16,1,128,640]{3,2,1,0:T(8,128)(2,1)}), bf16[16,1,128,640]{3,2,1,0:T(8,128)(2,1)S(1)}, u32[]{:S(2)}, u32[]{:S(2)}) %all-to-all-start.2) | async-done | bytes 2621472 | tf_op jit(solution)/shard_map/all_to_all | solution.py:72
  226.0 5.0 stack.3
  231.0 5.0 all-to-all-start.3
  239.2 284.0 %all-to-all-done.3 = bf16[16,512,640]{1,2,0:T(8,128)(2,1)} async-done(((bf16[16,512,640]{1,2,0:T(8,128)(2,1)}), bf16[16,512,640]{1,2,0:T(8,128)(2,1)}, u32[]{:S(2)}, u32[]{:S(2)}) %all-to-all-start.3) | async-done | bytes 10485792 | tf_op jit(solution)/shard_map/all_to_all | solution.py:121
  523.1 101.0 %all-gather.2.cloned.1.call-done = bf16[8192,640]{1,0:T(8,128)(2,1)} async-done(((bf16[512,640]{1,0:T(8,128)(2,1)}), bf16[8192,640]{1,0:T(8,128)(2,1)}) %all-gather.2.cloned.1.call-update) | async-done | bytes 10485776 | tf_op jit(solution)/shard_map/all_gather | solution.py:117
  624.1 198.0 %while.15 = (s32[]{:T(128)}, f32[5,512]{1,0:T(8,128)S(1)}, f32[5,512]{1,0:T(8,128)S(1)}, f32[512,5,128]{0,2,1:T(8,128)}, s32[512]{0:T(512)S(1)}, /*index=5*/s32[...) while((s32[]{:T(128)}, f32[5,512]{1,0:T(8,128)S(1)}, ...), condition=%wide.region_11.14_spmd.clone, body=%wide.region_8.0_spmd.clone.sunk | while | flops 689388544 | bytes 51683564 | solution.py:135
  630.6 4.5 fusion.47
  643.0 4.5 fusion.47
  655.3 4.5 fusion.47
  667.7 4.5 fusion.47
  680.1 4.5 fusion.47
  692.5 4.5 fusion.47
  704.9 4.5 fusion.47
  717.2 4.5 fusion.47
  729.6 4.5 fusion.47
  754.4 4.5 fusion.47
  766.8 4.5 fusion.47
  779.1 4.5 fusion.47
  791.5 4.5 fusion.47
  816.3 4.5 fusion.47
  827.7 9.2 %all-to-all-start.4 = ((bf16[16,1,128,640]{3,2,1,0:T(8,128)(2,1)}), bf16[16,1,128,640]{3,2,1,0:T(8,128)(2,1)S(1)}, u32[]{:S(2)}, u32[]{:S(2)}) async-start(bf16[16,1,128,640]{3,2,1,0:T(8,128)(2,1)} %fusion.17), calls=%async_computation.4 | async-start | bytes 5242880 | tf_op jit(solution)/shard_map/all_to_all | solution.py:143
  837.5 60.0 %all-to-all-done.4 = bf16[16,1,128,640]{3,2,1,0:T(8,128)(2,1)S(1)} async-done(((bf16[16,1,128,640]{3,2,1,0:T(8,128)(2,1)}), bf16[16,1,128,640]{3,2,1,0:T(8,128)(2,1)S(1)}, u32[]{:S(2)}, u32[]{:S(2)}) %all-to-all-start.4) | async-done | bytes 2621472 | tf_op jit(solution)/shard_map/all_to_all | solution.py:143
  (382 shorter events, 173.5 us)
Async XLA Ops:
  157.0 64.7 %all-to-all-start.2 = ((bf16[16,1,128,640]{3,2,1,0:T(8,128)(2,1)}), bf16[16,1,128,640]{3,2,1,0:T(8,128)(2,1)S(1)}, u32[]{:S(2)}, u32[]{:S(2)}) async-start(bf16[16,1,128,640]{3,2,1,0:T(8,128)(2,1)} %get-tuple-element.148), calls=%async_computation.2 | async-start | bytes 5242880 | tf_op jit(solution)/shard_map/all_to_all | solution.py:72
  231.0 6.2 copy-start.5
  231.0 292.1 %all-to-all-start.3 = ((bf16[16,512,640]{1,2,0:T(8,128)(2,1)}), bf16[16,512,640]{1,2,0:T(8,128)(2,1)}, u32[]{:S(2)}, u32[]{:S(2)}) async-start(bf16[16,512,640]{1,2,0:T(8,128)(2,1)} %stack.3), calls=%async_computation.3 | async-start | bytes 20971520 | tf_op jit(solution)/shard_map/all_to_all | solution.py:121
  236.0 388.1 %all-gather.2.cloned.1.call-start = ((), (), s32[]{:S(2)}) async-start(), calls=%async_computation.5 | async-start | bytes 11141120 | tf_op jit(solution)/shard_map/all_gather | solution.py:117
  625.8 4.8 copy-start.6
  629.3 5.9 slice-start
  641.6 5.8 slice-start
  654.0 5.8 slice-start
  666.4 5.8 slice-start
  678.8 5.8 slice-start
  691.2 5.8 slice-start
  700.0 4.8 copy-start.6
  703.5 5.8 slice-start
  715.9 5.8 slice-start
  728.3 5.8 slice-start
  740.7 5.8 slice-start
  753.1 5.8 slice-start
  765.4 5.8 slice-start
  777.8 5.8 slice-start
  790.2 5.8 slice-start
  802.6 5.8 slice-start
  814.9 5.8 slice-start
  827.7 69.8 %all-to-all-start.4 = ((bf16[16,1,128,640]{3,2,1,0:T(8,128)(2,1)}), bf16[16,1,128,640]{3,2,1,0:T(8,128)(2,1)S(1)}, u32[]{:S(2)}, u32[]{:S(2)}) async-start(bf16[16,1,128,640]{3,2,1,0:T(8,128)(2,1)} %fusion.17), calls=%async_computation.4 | async-start | bytes 5242880 | tf_op jit(solution)/shard_map/all_to_all | solution.py:143
  836.8 64.2 %copy-start.1 = (bf16[512,640]{1,0:T(8,128)(2,1)S(1)}, bf16[512,640]{1,0:T(8,128)(2,1)}, u32[]{:S(2)}) copy-start(bf16[512,640]{1,0:T(8,128)(2,1)} %param.11) | copy-start | bytes 1966084
  (51 other events, 173.7 us)
Sparse Core Ops, SparseCore 0:
  239.2 384.9 all-gather.1
